TPU v7x, 128 devices: a whole 4x4x4 slice. The times are simulated.
128 devices in a mesh: dp: 8 (over x_lo, y), expert: 16 (over x_hi, z, core).
Axes of the slice: x: 4 (x_hi: 2, x_lo: 2; x = x_hi * 2 + x_lo), y: 4, z: 4, core: 2. Of those that a mesh axis runs over, the one named last changes fastest.
Arguments:
- tokens: bfloat16 [65536, 2048], P(('dp', 'expert')), may hold values from -6 to 6
- probe: bfloat16 [65536, 2048], P(('dp', 'expert')), may hold values from -20 to 20
- domain: int32 [65536], P(('dp', 'expert')), may hold values from 0 to 21
- mix: float32 [22], replicated, may hold values from 0.5 to 2
- router: bfloat16 [2048, 32], replicated, may hold values from -0.125 to 0.125
- picks: int32 [128, 32, 40], P(('dp', 'expert')), may hold values from 0 to 511, as said below
- w_gate: bfloat16 [2048, 32, 768], P(None, 'expert'), may hold values from -0.125 to 0.125
- w_up: bfloat16 [2048, 32, 768], P(None, 'expert'), may hold values from -0.125 to 0.125
- w_down: bfloat16 [2048, 32, 768], P(None, 'expert'), may hold values from -0.21875 to 0.21875
Outputs:
- domain_loss: float32 [22], replicated
- router_grad: float32 [2048, 32], replicated
- grad_gate: bfloat16 [2048, 32, 768], P('dp', 'expert')
- grad_up: bfloat16 [2048, 32, 768], P('dp', 'expert')
- grad_down: bfloat16 [2048, 32, 768], P('dp', 'expert')
Inputs may be any that keep to these rules, and one draw needn't show every extreme that they name: The 40 picks of one expert on one device are distinct token positions of that device.
All inputs are finite; a program needn't handle non-finite values.
Results may differ from a plain program's by a relative error of at most 0.018.
Values may be sent and summed in bfloat16 or wider, within the bound.
A program may use at most 192 MiB of HBM per device.

v0:
```python
import math
import jax
import jax.numpy as jnp
from jax import lax
from jax.sharding import PartitionSpec as P

BF = jnp.bfloat16
F32 = jnp.float32


def body(tokens, probe, domain, mix, router, picks, w_gate, w_up, w_down):
    token_count, model_width = tokens.shape
    expert_count = router.shape[1]
    slot_count = picks.shape[2]
    pick_count = expert_count * slot_count
    domain_count = mix.shape[0]
    device_count = lax.axis_size("dp") * lax.axis_size("expert")
    flat = picks[0].reshape(pick_count)
    token_ids = jnp.arange(token_count, dtype=jnp.int32)
    select = (flat[:, None] == token_ids[None, :]).astype(BF)
    expert_of = jnp.repeat(jnp.arange(expert_count, dtype=jnp.int32), slot_count)
    own_expert = expert_of[:, None] == jnp.arange(expert_count, dtype=jnp.int32)[None, :]
    outgoing = jnp.dot(select, tokens, preferred_element_type=F32).astype(BF)
    received = lax.all_to_all(
        outgoing.reshape(expert_count, 1, slot_count, model_width),
        "expert",
        split_axis=0,
        concat_axis=1,
        tiled=True,
    )
    logits = jnp.dot(outgoing, router, preferred_element_type=F32)
    gate = jax.nn.sigmoid(jnp.sum(jnp.where(own_expert, logits, 0.0), axis=1))
    pre_gate = jnp.einsum("jsrd,djf->jsrf", received, w_gate, preferred_element_type=F32)
    pre_up = jnp.einsum("jsrd,djf->jsrf", received, w_up, preferred_element_type=F32)
    hidden = (jax.nn.silu(pre_gate) * pre_up).astype(BF)
    result = jnp.einsum("jsrf,djf->jsrd", hidden, w_down, preferred_element_type=F32).astype(BF)
    returned = lax.all_to_all(result, "expert", split_axis=1, concat_axis=0, tiled=True)
    returned = returned.reshape(pick_count, model_width)
    weighted = jnp.where(
        flat[None, :] == token_ids[:, None], gate.astype(BF)[None, :], jnp.zeros((), BF)
    )
    added = jnp.dot(weighted, returned, preferred_element_type=F32)
    difference = tokens.astype(F32) + added - probe.astype(F32)
    per_token = jnp.sum(difference * difference, axis=1)
    member = (domain[:, None] == jnp.arange(domain_count, dtype=jnp.int32)[None, :]).astype(F32)
    local_loss = jnp.sum(per_token[:, None] * member, axis=0)
    loss_scale = 1.0 / math.sqrt(device_count * slot_count)
    weight_tok = jnp.sum(member * mix[None, :], axis=1)
    upstream = ((loss_scale * weight_tok)[:, None] * difference).astype(BF)
    picked_up = jnp.dot(select, upstream, preferred_element_type=F32)
    sending = (gate[:, None] * picked_up).astype(BF)
    gate_slope = jnp.sum(picked_up * returned.astype(F32), axis=1)
    logit_grad = gate_slope * gate * (1.0 - gate)
    placing = jnp.where(own_expert, logit_grad[:, None], 0.0)
    high = placing.astype(BF)
    low = (placing - high.astype(F32)).astype(BF)
    placed = lax.dot_general(
        select,
        jnp.concatenate([high, low], axis=1),
        (((0,), (0,)), ((), ())),
        preferred_element_type=F32,
    ).astype(BF)
    router_part = lax.dot_general(
        tokens, placed, (((0,), (0,)), ((), ())), preferred_element_type=F32
    )
    router_part = router_part[:, :expert_count] + router_part[:, expert_count:]
    loss_rows = jnp.zeros((8, expert_count), F32).at[0, :domain_count].set(local_loss)
    summed = lax.psum(jnp.concatenate([router_part, loss_rows], axis=0), ("dp", "expert"))
    back_grad = lax.all_to_all(
        sending.reshape(expert_count, 1, slot_count, model_width),
        "expert",
        split_axis=0,
        concat_axis=1,
        tiled=True,
    )

    def reduced(left, right):
        part = jnp.einsum("jsrd,jsrf->djf", left, right, preferred_element_type=F32)
        return lax.psum_scatter(part.astype(BF), "dp", scatter_dimension=0, tiled=True)

    grad_down = reduced(back_grad, hidden)
    hidden_grad = jnp.einsum("jsrd,djf->jsrf", back_grad, w_down, preferred_element_type=F32)
    sigmoid_gate = jax.nn.sigmoid(pre_gate)
    gate_in = (
        hidden_grad * pre_up * sigmoid_gate * (1.0 + pre_gate * (1.0 - sigmoid_gate))
    ).astype(BF)
    up_in = (hidden_grad * (pre_gate * sigmoid_gate)).astype(BF)
    grad_gate = reduced(received, gate_in)
    grad_up = reduced(received, up_in)
    domain_loss = summed[model_width, :domain_count] * (
        domain_count / (token_count * device_count * model_width)
    )
    return (domain_loss, summed[:model_width], grad_gate, grad_up, grad_down)


def solution(mesh):
    placed = (
        P(("dp", "expert"), None),
        P(("dp", "expert"), None),
        P(("dp", "expert")),
        P(),
        P(),
        P(("dp", "expert"), None, None),
        P(None, "expert", None),
        P(None, "expert", None),
        P(None, "expert", None),
    )
    return jax.shard_map(
        body,
        mesh=mesh,
        in_specs=placed,
        out_specs=(
            P(),
            P(),
            P("dp", "expert", None),
            P("dp", "expert", None),
            P("dp", "expert", None),
        ),
        check_vma=False,
    )
```

profile of v0, /device:TPU:1, one launch (start us, length us, event | category | flops | bytes accessed | tf_op | source)
XLA Modules:
  0.0 530.8 jit_solution(12913081817586084446)
XLA Ops:
  8.9 4.9 convolution_convert_fusion
  13.8 71.2 %all_to_all.51 = bf16[32,1,40,2048]{3,2,1,0:T(8,128)(2,1)S(1)} all-to-all(bf16[32,1,40,2048]{3,2,1,0:T(8,128)(2,1)S(1)} %bitcast.69), channel_id=1, replica_groups=mesh['dp'=8,'expert'=16] {'expert'}, dimensions={0} | all-to-all | bytes 10485760 | tf_op jit(solution)/shard_map/all_to_all | solution.py:24
  85.0 4.4 fusion.5
  89.4 6.5 %multiply_convert_fusion.4 = (bf16[2,16,40,768]{3,2,1,0:T(8,128)(2,1)}, f32[2,16,40,768]{3,2,1,0:T(8,128)}) fusion(f32[2,16,40,768]{3,2,1,0:T(8,128)S(1)} %fusion.5, bf16[2048,2,768,1]{2,1,0,3:T(2,128)(2,1)S(1)} %bitcast.79, bf16[16,2,1,40,2048]{4,3,1,0,2:T(8,128)(2,1)S(1)} %bitcast.71), kind=kOutput, calls=%fused_computation.31 | convolution fusion | flops 4032430080 | bytes 21364736 | tf_op jit(solution)/shard_map/jsrd,djf->jsrf/dot_general | solution.py:34
  96.0 7.7 %fusion.19 = bf16[2,16,40,2048]{3,2,1,0:T(8,128)(2,1)S(1)} fusion(bf16[2,16,40,768]{3,2,1,0:T(8,128)(2,1)} %get-tuple-element.43, bf16[2048,2,768,1]{2,1,0,3:T(2,128)(2,1)} %bitcast.80), kind=kOutput, calls=%fused_computation.28 | convolution fusion | flops 4029153280 | bytes 13500416 | tf_op jit(solution)/shard_map/jsrf,djf->jsrd/dot_general | solution.py:36
  103.6 2.8 copy.51
  106.4 5.7 %all-to-all-start.1 = ((bf16[2,16,40,2048]{3,2,0,1:T(8,128)(2,1)}), bf16[2,16,40,2048]{3,2,0,1:T(8,128)(2,1)}, u32[]{:S(2)}, u32[]{:S(2)}) async-start(bf16[2,16,40,2048]{3,2,0,1:T(8,128)(2,1)} %copy.51), calls=%async_computation.1 | async-start | bytes 10485760 | tf_op jit(solution)/shard_map/all_to_all | solution.py:37
  112.2 4.3 fusion.38
  116.6 64.9 %all-to-all-done.1 = bf16[2,16,40,2048]{3,2,0,1:T(8,128)(2,1)} async-done(((bf16[2,16,40,2048]{3,2,0,1:T(8,128)(2,1)}), bf16[2,16,40,2048]{3,2,0,1:T(8,128)(2,1)}, u32[]{:S(2)}, u32[]{:S(2)}) %all-to-all-start.1) | async-done | bytes 5242912 | tf_op jit(solution)/shard_map/all_to_all | solution.py:37
  181.5 6.5 %multiply_reduce_fusion.1 = (f32[512]{0:T(512)S(1)}, f32[512,2048]{1,0:T(8,128)S(1)}) fusion(bf16[512,2048]{1,0:T(8,128)(2,1)} %param.12, bf16[1280,2048]{1,0:T(8,128)(2,1)} %bitcast.11, s32[1280]{0:T(1024)S(1)} %eq.64, bf16[1280]{0:T(1024)(128)(2,1)S(1)} %get-tuple-element.42, bf16[512,2048]{1,0:T(8,128)(2,1)S(1)} %copy-done.4), kind=kOutput, calls=%fused_computation.25 | convolution fusion | flops 2691956224 | bytes 13641216 | tf_op jit(solution)/shard_map/dot_general | solution.py:42
  188.1 7.4 %multiply_convert_fusion = (bf16[1280,2048]{1,0:T(8,128)(2,1)}, f32[1280]{0:T(1024)S(1)}) fusion(f32[1280]{0:T(1024)S(1)} %get-tuple-element.41, bf16[2,16,40,2048]{3,2,0,1:T(8,128)(2,1)} %all-to-all-done.1, f32[512,2048]{1,0:T(8,128)S(1)} %get-tuple-element.46, f32[512]{0:T(512)S(1)} %broadcast_multiply_fusion, s32[1280]{0:T(1024)S(1)} %eq.64), kind=kOutput, calls=%fused_computation.3 | convolution fusion | flops 2700212992 | bytes 14697472 | tf_op jit(solution)/shard_map/dot_general | solution.py:50
  195.5 14.7 %all-to-all-start.2 = ((bf16[32,1,40,2048]{3,2,1,0:T(8,128)(2,1)}), bf16[32,1,40,2048]{3,2,1,0:T(8,128)(2,1)}, u32[]{:S(2)}, u32[]{:S(2)}) async-start(bf16[32,1,40,2048]{3,2,1,0:T(8,128)(2,1)} %bitcast.74), calls=%async_computation.2 | async-start | bytes 10485760 | tf_op jit(solution)/shard_map/all_to_all | solution.py:69
  212.3 68.4 %all-to-all-done.2 = bf16[32,1,40,2048]{3,2,1,0:T(8,128)(2,1)} async-done(((bf16[32,1,40,2048]{3,2,1,0:T(8,128)(2,1)}), bf16[32,1,40,2048]{3,2,1,0:T(8,128)(2,1)}, u32[]{:S(2)}, u32[]{:S(2)}) %all-to-all-start.2) | async-done | bytes 5242912 | tf_op jit(solution)/shard_map/all_to_all | solution.py:69
  280.7 9.8 %fusion.2 = bf16[2048,2,768]{0,2,1:T(8,128)(2,1)} fusion(bf16[2,16,40,768]{3,2,1,0:T(8,128)(2,1)} %get-tuple-element.43, bf16[16,2,1,40,2048]{4,3,1,0,2:T(8,128)(2,1)} %bitcast.18), kind=kOutput, calls=%fused_computation.8 | convolution fusion | flops 4029677568 | bytes 13500416 | tf_op jit(solution)/shard_map/jsrd,jsrf->djf/dot_general | solution.py:78
  290.8 8.2 %fusion.7 = f32[2,16,40,768]{3,2,1,0:T(8,128)S(1)} fusion(bf16[2048,2,768,1]{2,1,0,3:T(2,128)(2,1)} %bitcast.81, bf16[16,2,1,40,2048]{4,3,1,0,2:T(8,128)(2,1)} %bitcast.18), kind=kOutput, calls=%fused_computation.13 | convolution fusion | flops 4026531840 | bytes 15466496 | tf_op jit(solution)/shard_map/jsrd,djf->jsrf/dot_general | solution.py:82
  299.0 1.8 copy-done.10
  300.9 9.9 %fusion.1 = bf16[2048,2,768]{0,2,1:T(8,128)(2,1)} fusion(bf16[16,2,1,40,2048]{4,3,1,0,2:T(8,128)(2,1)} %bitcast.72, f32[2,16,40,768]{3,2,1,0:T(8,128)S(1)} %fusion.7, f32[2,16,40,768]{3,2,1,0:T(8,128)S(1)} %copy-done.9), kind=kOutput, calls=%fused_computation.7 | convolution fusion | flops 4035575808 | bytes 19398656 | tf_op jit(solution)/shard_map/jsrd,jsrf->djf/dot_general | solution.py:78
  310.8 12.3 %fusion = bf16[2048,2,768]{0,2,1:T(8,128)(2,1)} fusion(bf16[16,2,1,40,2048]{4,3,1,0,2:T(8,128)(2,1)} %bitcast.73, f32[2,16,40,768]{3,2,1,0:T(8,128)} %copy-done.8, f32[2,16,40,768]{3,2,1,0:T(8,128)} %copy-done.10, f32[2,16,40,768]{3,2,1,0:T(8,128)} %get-tuple-element.44), kind=kOutput, calls=%fused_computation.6 | convolution fusion | flops 4039507968 | bytes 23330816 | tf_op jit(solution)/shard_map/jsrd,jsrf->djf/dot_general | solution.py:78
  323.2 129.6 %all-reduce.3.cloned.1.call-done = f32[2056,32]{0,1:T(8,128)} async-done(((f32[2056,32]{0,1:T(8,128)}), f32[2056,32]{0,1:T(8,128)}) %all-reduce.3.cloned.1.call-update) | async-done | bytes 263184 | tf_op jit(solution)/shard_map/psum | solution.py:68
  452.8 1.7 slice.35
  455.8 3.1 copy.58
  458.9 3.0 copy.57
  461.9 58.3 %reduce-scatter.4.cloned.1.call-done = bf16[256,2,768]{0,2,1:T(8,128)(2,1)} async-done(((bf16[2048,2,768]{0,2,1:T(8,128)(2,1)}), bf16[256,2,768]{0,2,1:T(8,128)(2,1)}) %reduce-scatter.4.cloned.1.call-update) | async-done | bytes 786448 | tf_op jit(solution)/shard_map/reduce_scatter | solution.py:79
  520.2 3.0 copy.56
  (50 shorter events, 4.9 us)
Async XLA Ops:
  8.0 104.2 %copy-start = (bf16[2048,32]{0,1:T(8,128)(2,1)S(1)}, bf16[2048,32]{0,1:T(8,128)(2,1)}, u32[]{:S(2)}) copy-start(bf16[2048,32]{0,1:T(8,128)(2,1)} %param.15) | copy-start | bytes 393220
  13.8 71.2 %copy-start.2 = (bf16[1280,2048]{1,0:T(8,128)(2,1)}, bf16[1280,2048]{1,0:T(8,128)(2,1)S(1)}, u32[]{:S(2)}) copy-start(bf16[1280,2048]{1,0:T(8,128)(2,1)S(1)} %convolution_convert_fusion) | copy-start | bytes 15728644
  13.8 71.2 %copy-start.7 = (bf16[2048,2,768]{2,1,0:T(2,128)(2,1)S(1)}, bf16[2048,2,768]{2,1,0:T(2,128)(2,1)}, u32[]{:S(2)}) copy-start(bf16[2048,2,768]{2,1,0:T(2,128)(2,1)} %param.17) | copy-start | bytes 18874372
  13.8 75.6 %slice-start = ((s8[6291456]{0:T(1024)(128)(4,1)}), s8[4194304]{0:T(1024)(128)(4,1)S(1)}, s32[]{:S(2)}) async-start(s8[6291456]{0:T(1024)(128)(4,1)} %bitcast.77), calls=%async_computation.10 | async-start | bytes 8388608
  85.0 4.4 copy-start.3
  85.0 4.4 slice-start.1
  89.4 6.6 %copy-start.8 = (f32[2,16,40,768]{3,2,1,0:T(8,128)}, f32[2,16,40,768]{3,2,1,0:T(8,128)S(1)}, u32[]{:S(2)}) copy-start(f32[2,16,40,768]{3,2,1,0:T(8,128)S(1)} %fusion.5) | copy-start | bytes 11796484
  106.4 75.0 %all-to-all-start.1 = ((bf16[2,16,40,2048]{3,2,0,1:T(8,128)(2,1)}), bf16[2,16,40,2048]{3,2,0,1:T(8,128)(2,1)}, u32[]{:S(2)}, u32[]{:S(2)}) async-start(bf16[2,16,40,2048]{3,2,0,1:T(8,128)(2,1)} %copy.51), calls=%async_computation.1 | async-start | bytes 10485760 | tf_op jit(solution)/shard_map/all_to_all | solution.py:37
  112.1 69.3 %copy-start.4 = (bf16[512,2048]{1,0:T(8,128)(2,1)S(1)}, bf16[512,2048]{1,0:T(8,128)(2,1)}, u32[]{:S(2)}) copy-start(bf16[512,2048]{1,0:T(8,128)(2,1)} %param.11) | copy-start | bytes 6291460
  181.5 6.5 %copy-start.5 = (s32[512]{0:T(512)S(1)}, s32[512]{0:T(512)}, u32[]{:S(2)}) copy-start(s32[512]{0:T(512)} %param.13) | copy-start | bytes 6148
  181.5 6.5 %copy-start.6 = (f32[22]{0:T(128)S(1)}, f32[22]{0:T(128)}, u32[]{:S(2)}) copy-start(f32[22]{0:T(128)} %param.14) | copy-start | bytes 268
  195.5 85.2 %all-to-all-start.2 = ((bf16[32,1,40,2048]{3,2,1,0:T(8,128)(2,1)}), bf16[32,1,40,2048]{3,2,1,0:T(8,128)(2,1)}, u32[]{:S(2)}, u32[]{:S(2)}) async-start(bf16[32,1,40,2048]{3,2,1,0:T(8,128)(2,1)} %bitcast.74), calls=%async_computation.2 | async-start | bytes 10485760 | tf_op jit(solution)/shard_map/all_to_all | solution.py:69
  210.2 242.6 %all-reduce.3.cloned.1.call-start = ((), (), s32[]{:S(2)}) async-start(), calls=%async_computation.6 | async-start | bytes 557056 | tf_op jit(solution)/shard_map/psum | solution.py:68
  212.2 243.5 %reduce-scatter.8.cloned.1.call-start = ((), (), s32[]{:S(2)}) async-start(), calls=%async_computation.9 | async-start | bytes 7077888 | tf_op jit(solution)/shard_map/reduce_scatter | solution.py:79
  290.5 168.3 %reduce-scatter.6.cloned.1.call-start = ((), (), s32[]{:S(2)}) async-start(), calls=%async_computation.8 | async-start | bytes 7077888 | tf_op jit(solution)/shard_map/reduce_scatter | solution.py:79
  290.8 10.1 %copy-start.9 = (f32[2,16,40,768]{3,2,1,0:T(8,128)S(1)}, f32[2,16,40,768]{3,2,1,0:T(8,128)}, u32[]{:S(2)}) copy-start(f32[2,16,40,768]{3,2,1,0:T(8,128)} %copy-done.8) | copy-start | bytes 11796484
  299.0 1.9 copy-start.10
  310.8 209.4 %reduce-scatter.4.cloned.1.call-start = ((), (), s32[]{:S(2)}) async-start(), calls=%async_computation.7 | async-start | bytes 7077888 | tf_op jit(solution)/shard_map/reduce_scatter | solution.py:79
  323.1 200.1 %copy-start.1 = (bf16[2048,32]{0,1:T(8,128)(2,1)S(1)}, bf16[2048,32]{0,1:T(8,128)(2,1)}, u32[]{:S(2)}) copy-start(bf16[2048,32]{0,1:T(8,128)(2,1)} %param.15) | copy-start | bytes 393220
Sparse Core Ops, SparseCore 0:
  216.3 236.3 all-reduce.2
Sparse Core Ops, SparseCore 1:
  290.6 81.2 reduce-scatter.7
  374.2 71.8 reduce-scatter.5
  448.3 71.9 reduce-scatter.3
where the time goes:
time: 531 us
  waiting for transfers between devices  321 us (60%)
  matrix products  82.8 us (16%)
  blocking collectives  71.2 us (13%)
  starting transfers between devices  20.8 us (4%)
  local copies, waits for them, and re-layouts  16.6 us (3%)
  between operations  15.9 us (3%)
    psum x1, waiting for transfers between devices, body(): lax.psum(jnp.concatenate([router_part, loss_rows], axis=0), ('dp', 'exper...  130 us
    all_to_all x1, blocking collectives, body(): lax.all_to_all(outgoing.reshape(expert_count, 1, slot_count, model_width)...  71.2 us
    all_to_all x1, waiting for transfers between devices, body(): lax.all_to_all(sending.reshape(expert_count, 1, slot_count, model_width),...  68.4 us
    all_to_all x1, waiting for transfers between devices, body(): lax.all_to_all(result, 'expert', split_axis=1, concat_axis=0, tiled=True)  64.9 us
    reduce_scatter x3, waiting for transfers between devices, reduced(): lax.psum_scatter(part.astype(BF), 'dp', scatter_dimension=0, tiled=True)  58.3 us
    dot_general x3, matrix products, reduced(): part = jnp.einsum('jsrd,jsrf->djf', left, right, preferred_element_type=F32)  32 us
    all_to_all x1, starting transfers between devices, body(): lax.all_to_all(sending.reshape(expert_count, 1, slot_count, model_width),...  14.7 us
    unnamed x29, local copies, waits for them, and re-layouts  11.1 us
  transfers between devices with their start and end apart: 6, of which 4 were waited for; matrix products, arithmetic and copies ran while one was open for 10% of the time, Pallas kernels for 0%

commit v1 on v0

--- a/solution.py
+++ b/solution.py
@@ -65,7 +65,9 @@
     )
     router_part = router_part[:, :expert_count] + router_part[:, expert_count:]
     loss_rows = jnp.zeros((8, expert_count), F32).at[0, :domain_count].set(local_loss)
-    summed = lax.psum(jnp.concatenate([router_part, loss_rows], axis=0), ("dp", "expert"))
+    summed = jnp.sum(
+        lax.all_gather(jnp.concatenate([router_part, loss_rows], axis=0), ("dp", "expert")), axis=0
+    )
     back_grad = lax.all_to_all(
         sending.reshape(expert_count, 1, slot_count, model_width),
         "expert",

time: 531 us -> 705 us (1.33)
  waiting for transfers between devices: 321 us -> 425 us
  blocking collectives: 71.2 us -> 148 us
  starting transfers between devices: 20.8 us -> 6.05 us
  other arithmetic: 2.29 us -> 13.7 us
    reduce_scatter x3, waiting for transfers between devices: 58.3 us -> 232 us  [reduced(): lax.psum_scatter(part.astype(BF), 'dp', scatter_dimension=0, tiled=True)]
    psum x1 -> x0, waiting for transfers between devices: 130 us -> none  [body(): lax.psum(jnp.concatenate([router_part, loss_rows], axis=0), ('dp', 'exper...]
    all_gather x0 -> x1, waiting for transfers between devices: none -> 128 us  [body(): lax.all_gather(jnp.concatenate([router_part, loss_rows], axis=0), ('dp',...]
    all_to_all x0 -> x1, blocking collectives: none -> 76.5 us  [body(): lax.all_to_all(sending.reshape(expert_count, 1, slot_count, model_width),...]
    all_to_all x1 -> x0, waiting for transfers between devices: 68.4 us -> none  [body(): lax.all_to_all(sending.reshape(expert_count, 1, slot_count, model_width),...]
    all_to_all x1 -> x0, starting transfers between devices: 14.7 us -> none  [body(): lax.all_to_all(sending.reshape(expert_count, 1, slot_count, model_width),...]
    reduce_sum x0 -> x1, other arithmetic: none -> 12.1 us  [body(): jnp.sum(lax.all_gather(jnp.concatenate([router_part, loss_rows], axis=0),...]
  transfers between devices with their start and end apart: 6 -> 5, of which waited for: 4 -> 5; matrix products, arithmetic and copies ran while one was open for 10% -> 7% of each run, Pallas kernels for 0% -> 0%
where the time goes in v1:
time: 705 us
  waiting for transfers between devices  425 us (60%)
  blocking collectives  148 us (21%)
  matrix products  78.8 us (11%)
  local copies, waits for them, and re-layouts  17.9 us (3%)
  between operations  15.4 us (2%)
  other arithmetic  13.7 us (2%)
    reduce_scatter x3, waiting for transfers between devices, reduced(): lax.psum_scatter(part.astype(BF), 'dp', scatter_dimension=0, tiled=True)  232 us
    all_gather x1, waiting for transfers between devices, body(): lax.all_gather(jnp.concatenate([router_part, loss_rows], axis=0), ('dp',...  128 us
    all_to_all x1, blocking collectives, body(): lax.all_to_all(sending.reshape(expert_count, 1, slot_count, model_width),...  76.5 us
    all_to_all x1, blocking collectives, body(): lax.all_to_all(outgoing.reshape(expert_count, 1, slot_count, model_width)...  71.2 us
    all_to_all x1, waiting for transfers between devices, body(): lax.all_to_all(result, 'expert', split_axis=1, concat_axis=0, tiled=True)  64.9 us
    dot_general x3, matrix products, reduced(): part = jnp.einsum('jsrd,jsrf->djf', left, right, preferred_element_type=F32)  29.4 us
  transfers between devices with their start and end apart: 5, of which 5 were waited for; matrix products, arithmetic and copies ran while one was open for 7% of the time, Pallas kernels for 0%

profile of v1, /device:TPU:1, one launch (start us, length us, event | category | flops | bytes accessed | tf_op | source)
XLA Modules:
  0.0 704.9 jit_solution(6079947111055324759)
XLA Ops:
  8.9 4.9 convolution_convert_fusion
  13.8 71.2 %all_to_all.51 = bf16[32,1,40,2048]{3,2,1,0:T(8,128)(2,1)S(1)} all-to-all(bf16[32,1,40,2048]{3,2,1,0:T(8,128)(2,1)S(1)} %bitcast.71), channel_id=1, replica_groups=mesh['dp'=8,'expert'=16] {'expert'}, dimensions={0} | all-to-all | bytes 10485760 | tf_op jit(solution)/shard_map/all_to_all | solution.py:24
  85.0 4.4 fusion.5
  89.4 6.5 multiply_convert_fusion.4
  96.0 7.7 %fusion.19 = bf16[2,16,40,2048]{3,2,1,0:T(8,128)(2,1)S(1)} fusion(bf16[2,16,40,768]{3,2,1,0:T(8,128)(2,1)} %get-tuple-element.43, bf16[2048,2,768,1]{2,1,0,3:T(2,128)(2,1)} %bitcast.84), kind=kOutput, calls=%fused_computation.28 | convolution fusion | flops 4029153280 | bytes 13500416 | tf_op jit(solution)/shard_map/jsrf,djf->jsrd/dot_general | solution.py:36
  103.7 2.7 copy.51
  106.4 5.7 all-to-all-start.1
  112.2 4.3 fusion.38
  116.5 64.9 %all-to-all-done.1 = bf16[2,16,40,2048]{3,2,0,1:T(8,128)(2,1)} async-done(((bf16[2,16,40,2048]{3,2,0,1:T(8,128)(2,1)}), bf16[2,16,40,2048]{3,2,0,1:T(8,128)(2,1)}, u32[]{:S(2)}, u32[]{:S(2)}) %all-to-all-start.1) | async-done | bytes 5242912 | tf_op jit(solution)/shard_map/all_to_all | solution.py:37
  181.4 6.5 multiply_reduce_fusion.1
  188.0 5.9 multiply_convert_fusion
  194.0 76.5 %all_to_all.52 = bf16[32,1,40,2048]{3,2,1,0:T(8,128)(2,1)S(1)} all-to-all(bf16[32,1,40,2048]{3,2,1,0:T(8,128)(2,1)S(1)} %bitcast.78), channel_id=1, replica_groups=mesh['dp'=8,'expert'=16] {'expert'}, dimensions={0} | all-to-all | bytes 10485760 | tf_op jit(solution)/shard_map/all_to_all | solution.py:71
  272.8 7.1 %fusion.2 = bf16[2048,2,768]{0,2,1:T(8,128)(2,1)} fusion(bf16[2,16,40,768]{3,2,1,0:T(8,128)(2,1)S(1)} %copy-done.12, bf16[16,2,1,40,2048]{4,3,1,0,2:T(8,128)(2,1)S(1)} %bitcast.76), kind=kOutput, calls=%fused_computation.8 | convolution fusion | flops 4029677568 | bytes 13500416 | tf_op jit(solution)/shard_map/jsrd,jsrf->djf/dot_general | solution.py:80
  280.2 8.2 %fusion.7 = f32[2,16,40,768]{3,2,1,0:T(8,128)S(1)} fusion(bf16[2048,2,768,1]{2,1,0,3:T(2,128)(2,1)} %bitcast.85, bf16[16,2,1,40,2048]{4,3,1,0,2:T(8,128)(2,1)} %bitcast.77), kind=kOutput, calls=%fused_computation.13 | convolution fusion | flops 4026531840 | bytes 15466496 | tf_op jit(solution)/shard_map/jsrd,djf->jsrf/dot_general | solution.py:84
  290.3 9.9 %fusion.1 = bf16[2048,2,768]{0,2,1:T(8,128)(2,1)} fusion(bf16[16,2,1,40,2048]{4,3,1,0,2:T(8,128)(2,1)} %bitcast.74, f32[2,16,40,768]{3,2,1,0:T(8,128)S(1)} %fusion.7, f32[2,16,40,768]{3,2,1,0:T(8,128)S(1)} %copy-done.10), kind=kOutput, calls=%fused_computation.7 | convolution fusion | flops 4035575808 | bytes 19398656 | tf_op jit(solution)/shard_map/jsrd,jsrf->djf/dot_general | solution.py:80
  300.2 12.4 %fusion = bf16[2048,2,768]{0,2,1:T(8,128)(2,1)} fusion(bf16[16,2,1,40,2048]{4,3,1,0,2:T(8,128)(2,1)} %bitcast.75, f32[2,16,40,768]{3,2,1,0:T(8,128)} %copy-done.9, f32[2,16,40,768]{3,2,1,0:T(8,128)} %copy-done.11, f32[2,16,40,768]{3,2,1,0:T(8,128)} %get-tuple-element.44), kind=kOutput, calls=%fused_computation.6 | convolution fusion | flops 4039507968 | bytes 23330816 | tf_op jit(solution)/shard_map/jsrd,jsrf->djf/dot_general | solution.py:80
  314.8 45.7 %reduce-scatter.8.cloned.1.call-done = bf16[256,2,768]{0,2,1:T(8,128)(2,1)} async-done(((bf16[2048,2,768]{0,2,1:T(8,128)(2,1)}), bf16[256,2,768]{0,2,1:T(8,128)(2,1)}) %reduce-scatter.8.cloned.1.call-update) | async-done | bytes 786448 | tf_op jit(solution)/shard_map/reduce_scatter | solution.py:81
  360.5 3.1 copy.58
  363.5 93.2 %reduce-scatter.6.cloned.1.call-done = bf16[256,2,768]{0,2,1:T(8,128)(2,1)} async-done(((bf16[2048,2,768]{0,2,1:T(8,128)(2,1)}), bf16[256,2,768]{0,2,1:T(8,128)(2,1)}) %reduce-scatter.6.cloned.1.call-update) | async-done | bytes 786448 | tf_op jit(solution)/shard_map/reduce_scatter | solution.py:81
  456.7 3.1 copy.57
  459.7 93.4 %reduce-scatter.4.cloned.1.call-done = bf16[256,2,768]{0,2,1:T(8,128)(2,1)} async-done(((bf16[2048,2,768]{0,2,1:T(8,128)(2,1)}), bf16[256,2,768]{0,2,1:T(8,128)(2,1)}) %reduce-scatter.4.cloned.1.call-update) | async-done | bytes 786448 | tf_op jit(solution)/shard_map/reduce_scatter | solution.py:81
  553.2 3.0 copy.56
  556.2 128.1 %all-gather.4.cloned.1.call-done = f32[128,2056,32]{1,2,0:T(8,128)} async-done(((f32[1,2056,32]{1,2,0:T(8,128)}), f32[128,2056,32]{1,2,0:T(8,128)}) %all-gather.4.cloned.1.call-update) | async-done | bytes 33685520 | tf_op jit(solution)/shard_map/all_gather | solution.py:69
  684.3 12.1 %reduce_sum.59 = f32[2056,32]{0,1:T(8,128)S(1)} reduce(f32[128,2056,32]{1,2,0:T(8,128)} %all-gather.4.cloned.1.call-done, f32[]{:T(128)} %constant.36.clone.1), dimensions={0}, to_apply=%region_5.6 | reduce | flops 8355584 | bytes 33948676 | tf_op jit(solution)/shard_map/reduce_sum | solution.py:68
  (54 shorter events, 9.1 us)
Async XLA Ops:
  8.0 104.2 %copy-start = (bf16[2048,32]{0,1:T(8,128)(2,1)S(1)}, bf16[2048,32]{0,1:T(8,128)(2,1)}, u32[]{:S(2)}) copy-start(bf16[2048,32]{0,1:T(8,128)(2,1)} %param.15) | copy-start | bytes 393220
  13.8 71.2 %copy-start.2 = (bf16[1280,2048]{1,0:T(8,128)(2,1)}, bf16[1280,2048]{1,0:T(8,128)(2,1)S(1)}, u32[]{:S(2)}) copy-start(bf16[1280,2048]{1,0:T(8,128)(2,1)S(1)} %convolution_convert_fusion) | copy-start | bytes 15728644
  13.8 71.2 %copy-start.8 = (bf16[2048,2,768]{2,1,0:T(2,128)(2,1)S(1)}, bf16[2048,2,768]{2,1,0:T(2,128)(2,1)}, u32[]{:S(2)}) copy-start(bf16[2048,2,768]{2,1,0:T(2,128)(2,1)} %param.17) | copy-start | bytes 18874372
  13.8 75.6 %slice-start = ((s8[6291456]{0:T(1024)(128)(4,1)}), s8[4194304]{0:T(1024)(128)(4,1)S(1)}, s32[]{:S(2)}) async-start(s8[6291456]{0:T(1024)(128)(4,1)} %bitcast.81), calls=%async_computation.10 | async-start | bytes 8388608
  85.0 4.4 copy-start.3
  85.0 4.4 slice-start.1
  89.4 6.6 copy-start.9
  106.4 75.0 %all-to-all-start.1 = ((bf16[2,16,40,2048]{3,2,0,1:T(8,128)(2,1)}), bf16[2,16,40,2048]{3,2,0,1:T(8,128)(2,1)}, u32[]{:S(2)}, u32[]{:S(2)}) async-start(bf16[2,16,40,2048]{3,2,0,1:T(8,128)(2,1)} %copy.51), calls=%async_computation.1 | async-start | bytes 10485760 | tf_op jit(solution)/shard_map/all_to_all | solution.py:37
  112.0 69.3 %copy-start.5 = (bf16[512,2048]{1,0:T(8,128)(2,1)S(1)}, bf16[512,2048]{1,0:T(8,128)(2,1)}, u32[]{:S(2)}) copy-start(bf16[512,2048]{1,0:T(8,128)(2,1)} %param.11) | copy-start | bytes 6291460
  112.0 248.4 %reduce-scatter.8.cloned.1.call-start = ((), (), s32[]{:S(2)}) async-start(), calls=%async_computation.8 | async-start | bytes 7077888 | tf_op jit(solution)/shard_map/reduce_scatter | solution.py:81
  181.4 6.5 copy-start.6
  181.4 6.5 copy-start.7
  194.0 78.8 %copy-start.12 = (bf16[2,16,40,768]{3,2,1,0:T(8,128)(2,1)S(1)}, bf16[2,16,40,768]{3,2,1,0:T(8,128)(2,1)}, u32[]{:S(2)}) copy-start(bf16[2,16,40,768]{3,2,1,0:T(8,128)(2,1)} %get-tuple-element.43) | copy-start | bytes 5898244
  270.4 2.3 copy-start.4
  279.9 176.8 %reduce-scatter.6.cloned.1.call-start = ((), (), s32[]{:S(2)}) async-start(), calls=%async_computation.7 | async-start | bytes 7077888 | tf_op jit(solution)/shard_map/reduce_scatter | solution.py:81
  280.2 10.1 %copy-start.10 = (f32[2,16,40,768]{3,2,1,0:T(8,128)S(1)}, f32[2,16,40,768]{3,2,1,0:T(8,128)}, u32[]{:S(2)}) copy-start(f32[2,16,40,768]{3,2,1,0:T(8,128)} %copy-done.9) | copy-start | bytes 11796484
  288.4 1.9 copy-start.11
  300.2 253.0 %reduce-scatter.4.cloned.1.call-start = ((), (), s32[]{:S(2)}) async-start(), calls=%async_computation.6 | async-start | bytes 7077888 | tf_op jit(solution)/shard_map/reduce_scatter | solution.py:81
  312.7 371.6 %all-gather.4.cloned.1.call-start = ((), (), s32[]{:S(2)}) async-start(), calls=%async_computation.9 | async-start | bytes 35930112 | tf_op jit(solution)/shard_map/all_gather | solution.py:69
  684.3 13.5 %copy-start.1 = (bf16[2048,32]{0,1:T(8,128)(2,1)S(1)}, bf16[2048,32]{0,1:T(8,128)(2,1)}, u32[]{:S(2)}) copy-start(bf16[2048,32]{0,1:T(8,128)(2,1)} %param.15) | copy-start | bytes 393220
Sparse Core Ops, SparseCore 0:
  280.0 80.4 reduce-scatter.7
  362.9 93.7 reduce-scatter.5
  459.1 94.0 reduce-scatter.3
Sparse Core Ops, SparseCore 1:
  314.9 369.3 all-gather.3
